TPU v7x, 32 devices: a whole 2x2x4 slice. The times are simulated.
32 devices in a mesh: seq: 16 (over z, y, core), head: 2 (over x).
Axes of the slice: x: 2, y: 2, z: 4, core: 2. Of those that a mesh axis runs over, the one named last changes fastest.
Arguments:
- queries: bfloat16 [4, 64, 64, 128], P(None, None, 'head'), may hold values from -15 to 15
- new_keys: bfloat16 [4, 64, 8, 128], P(None, None, 'head'), may hold values from -16 to 16
- new_values: bfloat16 [4, 64, 8, 128], P(None, None, 'head'), may hold values from -6 to 6
- cache_keys: bfloat16 [4, 32768, 8, 128], P(None, 'seq', 'head'), may hold values from -6 to 6
- cache_values: bfloat16 [4, 32768, 8, 128], P(None, 'seq', 'head'), may hold values from -6 to 6
- parents: int32 [4, 64], replicated, may hold values from 0 to 63, as said below
- kv_lengths: int32 [4], replicated, may hold values from 1 to 32768
- out_weight: bfloat16 [8192, 8192], P('head', 'seq'), may hold values from -0.5 to 0.5
Outputs:
- mixed: bfloat16 [256, 8192], P('head', 'seq')
Inputs may be any that keep to these rules, and one draw needn't show every extreme that they name: parents[r, 0] = 0 for the root; for i >= 1, parents[r, i] < i.
All inputs are finite; a program needn't handle non-finite values.
Results may differ from a plain program's by a relative error of at most 0.0045.
Values may be sent and summed in bfloat16 or wider, within the bound.
A program may use at most 128 MiB of HBM per device.

v0:
```python
import math
import jax
import jax.numpy as jnp
from jax import lax
from jax.sharding import PartitionSpec as P

lowest = -1e30


def ancestors(parent_row):
    tree_size = parent_row.shape[0]
    indices = jnp.arange(tree_size, dtype=jnp.int32)
    parent_link = (parent_row[:, None] == indices[None, :]).astype(jnp.float32)
    itself = (indices[:, None] == indices[None, :]).astype(jnp.float32)
    reached = jnp.maximum(parent_link, itself)
    for repeat in range(max(1, (tree_size - 1).bit_length())):
        reached = jnp.minimum(jnp.dot(reached, reached, precision=lax.Precision.HIGHEST), 1.0)
    return reached


def partial_scores(query_rows, keys, values, allowed, score_scale):
    scores = (
        jnp.einsum("kqd,pkd->kqp", query_rows, keys, preferred_element_type=jnp.float32)
        * score_scale
    )
    scores = jnp.where(allowed, scores, lowest)
    maxima = jnp.max(scores, axis=-1)
    weights = jnp.where(allowed, jnp.exp(scores - maxima[..., None]), 0.0)
    totals = jnp.sum(weights, axis=-1)
    weighted = jnp.einsum(
        "kqp,pkd->kqd", weights.astype(jnp.bfloat16), values, preferred_element_type=jnp.float32
    )
    return (maxima, totals, weighted)


def body(queries, new_keys, new_values, cache_keys, cache_values, parents, kv_lengths, out_weight):
    requests, tree_size, heads, head_size = queries.shape
    kv_heads = new_keys.shape[2]
    group_size = heads // kv_heads
    block_size = cache_keys.shape[1]
    score_scale = 1.0 / math.sqrt(head_size)
    tokens = requests * tree_size
    positions = lax.axis_index("seq") * block_size + jnp.arange(block_size, dtype=jnp.int32)

    def token_order(maxima, totals, weighted):
        maxima = (
            maxima.reshape(kv_heads, tree_size, group_size)
            .transpose(1, 0, 2)
            .reshape(tree_size, heads)
        )
        totals = (
            totals.reshape(kv_heads, tree_size, group_size)
            .transpose(1, 0, 2)
            .reshape(tree_size, heads)
        )
        weighted = weighted.reshape(kv_heads, tree_size, group_size, head_size).transpose(
            1, 0, 2, 3
        )
        return (maxima, totals, weighted.reshape(tree_size, heads, head_size))

    def one_request(request_items):
        query, tree_keys, tree_values, past_keys, past_values, parent_row, length = request_items
        query_rows = query.reshape(tree_size, kv_heads, group_size, head_size).transpose(1, 0, 2, 3)
        query_rows = query_rows.reshape(kv_heads, tree_size * group_size, head_size)
        cache_max, cache_tot, cache_acc = partial_scores(
            query_rows, past_keys, past_values, positions < length, score_scale
        )
        tree_allowed = jnp.repeat(ancestors(parent_row), group_size, axis=0) > 0.5
        tree_max, tree_tot, tree_acc = partial_scores(
            query_rows, tree_keys, tree_values, tree_allowed, score_scale
        )
        return (
            token_order(cache_max, cache_tot, cache_acc),
            token_order(tree_max, tree_tot, tree_acc),
        )

    cache_part, tree_part = lax.map(
        one_request, (queries, new_keys, new_values, cache_keys, cache_values, parents, kv_lengths)
    )
    cache_max = cache_part[0].reshape(tokens, heads)
    cache_tot = cache_part[1].reshape(tokens, heads)
    cache_acc = cache_part[2].reshape(tokens, heads, head_size)
    tree_max = tree_part[0].reshape(tokens, heads)
    tree_tot = tree_part[1].reshape(tokens, heads)
    tree_acc = tree_part[2].reshape(tokens, heads, head_size)
    overall = lax.pmax(cache_max, "seq")
    overall = jnp.maximum(overall, tree_max)
    factor = jnp.exp(cache_max - overall)
    shared_acc, shared_tot = (
        lax.psum_scatter(cache_acc * factor[..., None], "seq", scatter_dimension=0, tiled=True),
        lax.psum_scatter(cache_tot * factor, "seq", scatter_dimension=0, tiled=True),
    )
    row_count = tokens // lax.axis_size("seq")
    first_row = lax.axis_index("seq") * row_count

    def take_rows(array):
        return lax.dynamic_slice_in_dim(array, first_row, row_count, 0)

    tree_factor = jnp.exp(take_rows(tree_max) - take_rows(overall))
    weighted = shared_acc + take_rows(tree_acc) * tree_factor[..., None]
    totals = shared_tot + take_rows(tree_tot) * tree_factor
    share = (
        (weighted / totals[..., None]).astype(jnp.bfloat16).reshape(row_count, heads * head_size)
    )
    attended = lax.all_gather(share, "seq", axis=0, tiled=True)
    mixed = lax.psum_scatter(
        jnp.dot(attended, out_weight, preferred_element_type=jnp.float32),
        "head",
        scatter_dimension=0,
        tiled=True,
    )
    return mixed.astype(jnp.bfloat16)


def solution(mesh):
    placed = (
        P(None, None, "head", None),
        P(None, None, "head", None),
        P(None, None, "head", None),
        P(None, "seq", "head", None),
        P(None, "seq", "head", None),
        P(),
        P(),
        P("head", "seq"),
    )
    return jax.shard_map(
        body, mesh=mesh, in_specs=placed, out_specs=P("head", "seq"), check_vma=False
    )
```

profile of v0, /device:TPU:0, one launch (start us, length us, event | category | flops | bytes accessed | tf_op | source)
XLA Modules:
  0.0 414.5 jit_solution(2779970047454667348)
XLA Ops:
  6.5 145.8 %while.21 = (s32[]{:T(128)}, f32[4,64,32]{1,0,2:T(4,128)S(1)}, f32[4,64,32]{1,0,2:T(4,128)S(1)}, f32[4,64,32,128]{3,2,1,0:T(8,128)}, f32[4,64,32]{1,0,2:T(4,128)...) while((s32[]{:T(128)}, f32[4,64,32]{1,0,2:T(4,128)S(1)}, ...), condition=%wide.region_5.6_spmd.clone, body=%wide.region_0.5_spmd.clone.sunk | while | flops 2289217536 | bytes 81249280 | solution.py:77
  8.7 2.0 constant_dynamic-slice_fusion.9
  10.7 7.2 %fusion.81 = (f32[4,512]{1,0:T(4,128)S(1)}, f32[4,512,2048]{2,1,0:T(8,128)}) fusion(pred[2048]{0:T(1024)(128)(4,1)S(1)} %add_compare_fusion.2, bf16[1,2048,4,128]{3,2,1,0:T(4,128)(2,1)S(1)} %constant_dynamic-slice_fusion.9, bf16[4,64,32,128]{3,2,1,0:T(8,128)(2,1)S(1)} %copy-done, s32[]{:T(128)S(6)} %copy.150), kind=kOutput, calls=%fused_computation.3.clone.1 | convolution fusion | flops 1086322688 | bytes 19408900 | tf_op jit(solution)/shard_map/while/body/eval_jaxpr/kqd,pkd->kqp/dot_general | solution.py:23
  18.2 8.1 %fusion.82 = f32[4,512]{1,0:T(4,128)S(1)} fusion(f32[4,512,2048]{2,1,0:T(8,128)} %get-tuple-element.325, f32[4,512]{1,0:T(4,128)S(1)} %get-tuple-element.324, pred[2048]{0:T(1024)(128)(4,1)S(1)} %add_compare_fusion.2), kind=kLoop, calls=%fused_computation.5.clone.1 | loop fusion | flops 20969472 | bytes 16795648 | tf_op jit(solution)/shard_map/while/body/eval_jaxpr/reduce_sum | solution.py:29
  31.0 2.0 constant_dynamic-slice_fusion.12
  33.0 7.7 %fusion.86 = f32[64,4,8,128]{3,2,0,1:T(8,128)S(1)} fusion(bf16[1,2048,4,128]{3,2,1,0:T(4,128)(2,1)S(1)} %constant_dynamic-slice_fusion.12, f32[4,512,2048]{2,1,0:T(8,128)} %get-tuple-element.325, f32[4,512]{1,0:T(4,128)S(1)} %get-tuple-element.324, pred[2048]{0:T(1024)(128)(4,1)S(1)} %add_compare_fusion.2), kind=kOutput, calls=%fused_computation.11.clone.1 | convolution fusion | flops 1094713344 | bytes 19933184 | tf_op jit(solution)/shard_map/while/body/eval_jaxpr/kqp,pkd->kqd/dot_general | solution.py:30
  45.2 2.0 constant_dynamic-slice_fusion.9
  47.2 7.2 %fusion.81 = (f32[4,512]{1,0:T(4,128)S(1)}, f32[4,512,2048]{2,1,0:T(8,128)}) fusion(pred[2048]{0:T(1024)(128)(4,1)S(1)} %add_compare_fusion.2, bf16[1,2048,4,128]{3,2,1,0:T(4,128)(2,1)S(1)} %constant_dynamic-slice_fusion.9, bf16[4,64,32,128]{3,2,1,0:T(8,128)(2,1)S(1)} %copy-done, s32[]{:T(128)S(6)} %copy.150), kind=kOutput, calls=%fused_computation.3.clone.1 | convolution fusion | flops 1086322688 | bytes 19408900 | tf_op jit(solution)/shard_map/while/body/eval_jaxpr/kqd,pkd->kqp/dot_general | solution.py:23
  54.7 8.1 %fusion.82 = f32[4,512]{1,0:T(4,128)S(1)} fusion(f32[4,512,2048]{2,1,0:T(8,128)} %get-tuple-element.325, f32[4,512]{1,0:T(4,128)S(1)} %get-tuple-element.324, pred[2048]{0:T(1024)(128)(4,1)S(1)} %add_compare_fusion.2), kind=kLoop, calls=%fused_computation.5.clone.1 | loop fusion | flops 20969472 | bytes 16795648 | tf_op jit(solution)/shard_map/while/body/eval_jaxpr/reduce_sum | solution.py:29
  67.5 2.0 constant_dynamic-slice_fusion.12
  69.5 7.7 %fusion.86 = f32[64,4,8,128]{3,2,0,1:T(8,128)S(1)} fusion(bf16[1,2048,4,128]{3,2,1,0:T(4,128)(2,1)S(1)} %constant_dynamic-slice_fusion.12, f32[4,512,2048]{2,1,0:T(8,128)} %get-tuple-element.325, f32[4,512]{1,0:T(4,128)S(1)} %get-tuple-element.324, pred[2048]{0:T(1024)(128)(4,1)S(1)} %add_compare_fusion.2), kind=kOutput, calls=%fused_computation.11.clone.1 | convolution fusion | flops 1094713344 | bytes 19933184 | tf_op jit(solution)/shard_map/while/body/eval_jaxpr/kqp,pkd->kqd/dot_general | solution.py:30
  83.7 7.2 %fusion.81 = (f32[4,512]{1,0:T(4,128)S(1)}, f32[4,512,2048]{2,1,0:T(8,128)}) fusion(pred[2048]{0:T(1024)(128)(4,1)S(1)} %add_compare_fusion.2, bf16[1,2048,4,128]{3,2,1,0:T(4,128)(2,1)S(1)} %constant_dynamic-slice_fusion.9, bf16[4,64,32,128]{3,2,1,0:T(8,128)(2,1)S(1)} %copy-done, s32[]{:T(128)S(6)} %copy.150), kind=kOutput, calls=%fused_computation.3.clone.1 | convolution fusion | flops 1086322688 | bytes 19408900 | tf_op jit(solution)/shard_map/while/body/eval_jaxpr/kqd,pkd->kqp/dot_general | solution.py:23
  91.2 8.1 %fusion.82 = f32[4,512]{1,0:T(4,128)S(1)} fusion(f32[4,512,2048]{2,1,0:T(8,128)} %get-tuple-element.325, f32[4,512]{1,0:T(4,128)S(1)} %get-tuple-element.324, pred[2048]{0:T(1024)(128)(4,1)S(1)} %add_compare_fusion.2), kind=kLoop, calls=%fused_computation.5.clone.1 | loop fusion | flops 20969472 | bytes 16795648 | tf_op jit(solution)/shard_map/while/body/eval_jaxpr/reduce_sum | solution.py:29
  105.9 7.7 %fusion.86 = f32[64,4,8,128]{3,2,0,1:T(8,128)S(1)} fusion(bf16[1,2048,4,128]{3,2,1,0:T(4,128)(2,1)S(1)} %constant_dynamic-slice_fusion.12, f32[4,512,2048]{2,1,0:T(8,128)} %get-tuple-element.325, f32[4,512]{1,0:T(4,128)S(1)} %get-tuple-element.324, pred[2048]{0:T(1024)(128)(4,1)S(1)} %add_compare_fusion.2), kind=kOutput, calls=%fused_computation.11.clone.1 | convolution fusion | flops 1094713344 | bytes 19933184 | tf_op jit(solution)/shard_map/while/body/eval_jaxpr/kqp,pkd->kqd/dot_general | solution.py:30
  120.1 7.2 %fusion.81 = (f32[4,512]{1,0:T(4,128)S(1)}, f32[4,512,2048]{2,1,0:T(8,128)}) fusion(pred[2048]{0:T(1024)(128)(4,1)S(1)} %add_compare_fusion.2, bf16[1,2048,4,128]{3,2,1,0:T(4,128)(2,1)S(1)} %constant_dynamic-slice_fusion.9, bf16[4,64,32,128]{3,2,1,0:T(8,128)(2,1)S(1)} %copy-done, s32[]{:T(128)S(6)} %copy.150), kind=kOutput, calls=%fused_computation.3.clone.1 | convolution fusion | flops 1086322688 | bytes 19408900 | tf_op jit(solution)/shard_map/while/body/eval_jaxpr/kqd,pkd->kqp/dot_general | solution.py:23
  127.6 8.1 %fusion.82 = f32[4,512]{1,0:T(4,128)S(1)} fusion(f32[4,512,2048]{2,1,0:T(8,128)} %get-tuple-element.325, f32[4,512]{1,0:T(4,128)S(1)} %get-tuple-element.324, pred[2048]{0:T(1024)(128)(4,1)S(1)} %add_compare_fusion.2), kind=kLoop, calls=%fused_computation.5.clone.1 | loop fusion | flops 20969472 | bytes 16795648 | tf_op jit(solution)/shard_map/while/body/eval_jaxpr/reduce_sum | solution.py:29
  142.4 7.7 %fusion.86 = f32[64,4,8,128]{3,2,0,1:T(8,128)S(1)} fusion(bf16[1,2048,4,128]{3,2,1,0:T(4,128)(2,1)S(1)} %constant_dynamic-slice_fusion.12, f32[4,512,2048]{2,1,0:T(8,128)} %get-tuple-element.325, f32[4,512]{1,0:T(4,128)S(1)} %get-tuple-element.324, pred[2048]{0:T(1024)(128)(4,1)S(1)} %add_compare_fusion.2), kind=kOutput, calls=%fused_computation.11.clone.1 | convolution fusion | flops 1094713344 | bytes 19933184 | tf_op jit(solution)/shard_map/while/body/eval_jaxpr/kqp,pkd->kqd/dot_general | solution.py:30
  152.6 63.0 %pmax.7 = f32[256,32]{0,1:T(8,128)S(1)} all-reduce(f32[256,32]{0,1:T(8,128)S(1)} %reshape.69), channel_id=1, replica_groups=mesh['seq'=16,'head'=2] {'seq'}, use_global_device_ids=true, to_apply=%region_6.7 | all-reduce | flops 8192 | bytes 65536 | tf_op jit(solution)/shard_map/pmax | solution.py:86
  216.6 4.1 %bitcast_multiply_fusion = f32[256,32,128]{2,1,0:T(8,128)} fusion(f32[4,64,32,128]{3,2,1,0:T(8,128)} %get-tuple-element.87, f32[256,32]{1,0:T(8,128)S(1)} %copy.63), kind=kLoop, calls=%fused_computation.55 | loop fusion | flops 1048576 | bytes 8421376 | tf_op jit(solution)/shard_map/mul | solution.py:90
  221.0 48.6 %reduce-scatter.10.cloned.1.call-done = f32[16,32]{1,0:T(8,128)} async-done(((f32[256,32]{1,0:T(8,128)}), f32[16,32]{1,0:T(8,128)}) %reduce-scatter.10.cloned.1.call-update) | async-done | bytes 2064
  270.5 74.7 %reduce-scatter.6.cloned.1.call-done = f32[16,32,128]{2,1,0:T(8,128)} async-done(((f32[256,32,128]{2,1,0:T(8,128)}), f32[16,32,128]{2,1,0:T(8,128)}) %reduce-scatter.6.cloned.1.call-update) | async-done | bytes 262160 | tf_op jit(solution)/shard_map/reduce_scatter | solution.py:90
  347.2 40.7 %all-gather.2.cloned.1.call-done = bf16[256,4096]{1,0:T(8,128)(2,1)} async-done(((bf16[16,4096]{1,0:T(8,128)(2,1)}), bf16[256,4096]{1,0:T(8,128)(2,1)}) %all-gather.2.cloned.1.call-update) | async-done | bytes 2097168 | tf_op jit(solution)/shard_map/all_gather | solution.py:105
  387.9 4.9 %fusion.35 = f32[256,512]{1,0:T(8,128)} fusion(bf16[256,4096]{1,0:T(8,128)(2,1)} %all-gather.2.cloned.1.call-done, bf16[4096,512]{1,0:T(8,128)(2,1)} %param.17), kind=kOutput, calls=%fused_computation.63 | convolution fusion | flops 1073741824 | bytes 6815744 | tf_op jit(solution)/shard_map/dot_general | solution.py:107
  392.8 13.5 %reduce-scatter.8.cloned.1.call-done = f32[128,512]{1,0:T(8,128)} async-done(((f32[256,512]{1,0:T(8,128)}), f32[128,512]{1,0:T(8,128)}) %reduce-scatter.8.cloned.1.call-update) | async-done | bytes 262160 | tf_op jit(solution)/shard_map/reduce_scatter | solution.py:106
  (156 shorter events, 51.4 us)
Async XLA Ops:
  6.5 263.0 %reduce-scatter.10.cloned.1.call-start = ((), (), s32[]{:S(2)}) async-start(), calls=%async_computation.6 | async-start | bytes 139264
  6.6 4.2 %copy-start = (bf16[4,64,32,128]{3,2,1,0:T(8,128)(2,1)S(1)}, bf16[4,64,32,128]{3,2,1,0:T(8,128)(2,1)}, u32[]{:S(2)}) copy-start(bf16[4,64,32,128]{3,2,1,0:T(8,128)(2,1)} %get-tuple-element.372) | copy-start | bytes 6291460 | tf_op jit(solution)/shard_map/while
  43.0 4.2 %copy-start = (bf16[4,64,32,128]{3,2,1,0:T(8,128)(2,1)S(1)}, bf16[4,64,32,128]{3,2,1,0:T(8,128)(2,1)}, u32[]{:S(2)}) copy-start(bf16[4,64,32,128]{3,2,1,0:T(8,128)(2,1)} %get-tuple-element.372) | copy-start | bytes 6291460 | tf_op jit(solution)/shard_map/while
  79.5 4.2 %copy-start = (bf16[4,64,32,128]{3,2,1,0:T(8,128)(2,1)S(1)}, bf16[4,64,32,128]{3,2,1,0:T(8,128)(2,1)}, u32[]{:S(2)}) copy-start(bf16[4,64,32,128]{3,2,1,0:T(8,128)(2,1)} %get-tuple-element.372) | copy-start | bytes 6291460 | tf_op jit(solution)/shard_map/while
  116.0 4.2 %copy-start = (bf16[4,64,32,128]{3,2,1,0:T(8,128)(2,1)S(1)}, bf16[4,64,32,128]{3,2,1,0:T(8,128)(2,1)}, u32[]{:S(2)}) copy-start(bf16[4,64,32,128]{3,2,1,0:T(8,128)(2,1)} %get-tuple-element.372) | copy-start | bytes 6291460 | tf_op jit(solution)/shard_map/while
  216.5 128.7 %reduce-scatter.6.cloned.1.call-start = ((), (), s32[]{:S(2)}) async-start(), calls=%async_computation.3 | async-start | bytes 4456448 | tf_op jit(solution)/shard_map/reduce_scatter | solution.py:90
  220.8 167.1 %all-gather.2.cloned.1.call-start = ((), (), s32[]{:S(2)}) async-start(), calls=%async_computation.4 | async-start | bytes 2228224 | tf_op jit(solution)/shard_map/all_gather | solution.py:105
  347.2 59.1 %reduce-scatter.8.cloned.1.call-start = ((), (), s32[]{:S(2)}) async-start(), calls=%async_computation.5 | async-start | bytes 786432 | tf_op jit(solution)/shard_map/reduce_scatter | solution.py:106
Sparse Core Ops, SparseCore 0:
  216.6 52.8 reduce-scatter.9
  273.4 71.7 reduce-scatter.5
  347.4 40.4 all-gather.1
  392.9 13.3 reduce-scatter.7
where the time goes:
time: 416 us; the launch traced here: 414 us
  waiting for transfers between devices  178 us (43%)
  matrix products  71.1 us (17%)
  blocking collectives  63 us (15%)
  local copies, waits for them, and re-layouts  46 us (11%)
  other arithmetic  42.7 us (10%)
  between operations  13.2 us (3%)
    reduce_scatter x1, waiting for transfers between devices, body(): lax.psum_scatter(cache_acc * factor[..., None], 'seq', scatter_dimension=...  74.7 us
    pmax x1, blocking collectives, body(): overall = lax.pmax(cache_max, 'seq')  63 us
    unnamed x5, waiting for transfers between devices  48.6 us
    all_gather x1, waiting for transfers between devices, body(): attended = lax.all_gather(share, 'seq', axis=0, tiled=True)  40.7 us
    reduce_sum x8, other arithmetic, partial_scores(): totals = jnp.sum(weights, axis=-1)  32.9 us
    dot_general x8, matrix products, partial_scores(): jnp.einsum('kqp,pkd->kqd', weights.astype(jnp.bfloat16), values, preferre...  32.1 us
    dot_general x8, matrix products, partial_scores(): jnp.einsum('kqd,pkd->kqp', query_rows, keys, preferred_element_type=jnp.f...  30 us
    dynamic_slice x20, local copies, waits for them, and re-layouts, body(): lax.map(one_request, (queries, new_keys, new_values, cache_keys, cache_va...  28.8 us
  transfers between devices with their start and end apart: 4, of which 4 were waited for; matrix products, arithmetic and copies ran while one was open for 1% of the time, Pallas kernels for 0%

commit v1 on v0

--- a/solution.py
+++ b/solution.py
@@ -5,6 +5,17 @@
 from jax.sharding import PartitionSpec as P
 
 lowest = -1e30
+
+
+def gather_by_hops(x, axis, dim):
+    peers = lax.axis_size(axis)
+    right = [(i, (i + 1) % peers) for i in range(peers)]
+    blocks = [x]
+    for far in range(1, peers):
+        blocks = [lax.ppermute(blocks[0], axis, right), *blocks]
+    result = jnp.concatenate(blocks, axis=dim)
+    shift = (lax.axis_index(axis) + 1) * blocks[-1].shape[dim]
+    return jnp.roll(result, shift, axis=dim)
 
 
 def ancestors(parent_row):
@@ -102,7 +113,7 @@
     share = (
         (weighted / totals[..., None]).astype(jnp.bfloat16).reshape(row_count, heads * head_size)
     )
-    attended = lax.all_gather(share, "seq", axis=0, tiled=True)
+    attended = gather_by_hops(share, "seq", 0)
     mixed = lax.psum_scatter(
         jnp.dot(attended, out_weight, preferred_element_type=jnp.float32),
         "head",

time: 416 us -> 477 us (1.15)
  waiting for transfers between devices: 178 us -> 242 us
    ppermute x0 -> x15, waiting for transfers between devices: none -> 106 us  [gather_by_hops(): blocks = [lax.ppermute(blocks[0], axis, right), *blocks]]
    all_gather x1 -> x0, waiting for transfers between devices: 40.7 us -> none  [body(): attended = lax.all_gather(share, 'seq', axis=0, tiled=True)]
    unnamed x5 -> x4, waiting for transfers between devices: 48.6 us -> 48.6 us
  transfers between devices with their start and end apart: 4 -> 18, of which waited for: 4 -> 18; matrix products, arithmetic and copies ran while one was open for 1% -> 1% of each run, Pallas kernels for 0% -> 0%
where the time goes in v1:
time: 477 us; the launch traced here: 476 us
  waiting for transfers between devices  242 us (51%)
  matrix products  68.4 us (14%)
  blocking collectives  63 us (13%)
  local copies, waits for them, and re-layouts  45.7 us (10%)
  other arithmetic  42.7 us (9%)
  between operations  13.4 us (3%)
    ppermute x15, waiting for transfers between devices, gather_by_hops(): blocks = [lax.ppermute(blocks[0], axis, right), *blocks]  106 us
    reduce_scatter x1, waiting for transfers between devices, body(): lax.psum_scatter(cache_acc * factor[..., None], 'seq', scatter_dimension=...  74.8 us
    pmax x1, blocking collectives, body(): overall = lax.pmax(cache_max, 'seq')  63 us
    unnamed x4, waiting for transfers between devices  48.6 us
    reduce_sum x8, other arithmetic, partial_scores(): totals = jnp.sum(weights, axis=-1)  32.9 us
    dot_general x8, matrix products, partial_scores(): jnp.einsum('kqp,pkd->kqd', weights.astype(jnp.bfloat16), values, preferre...  32.1 us
    dot_general x8, matrix products, partial_scores(): jnp.einsum('kqd,pkd->kqp', query_rows, keys, preferred_element_type=jnp.f...  30.1 us
    dynamic_slice x20, local copies, waits for them, and re-layouts, body(): lax.map(one_request, (queries, new_keys, new_values, cache_keys, cache_va...  28.7 us
  transfers between devices with their start and end apart: 18, of which 18 were waited for; matrix products, arithmetic and copies ran while one was open for 1% of the time, Pallas kernels for 0%

profile of v1, /device:TPU:0, one launch (start us, length us, event | category | flops | bytes accessed | tf_op | source)
XLA Modules:
  0.0 475.9 jit_solution(11823134101304719582)
XLA Ops:
  6.5 145.9 %while.21 = (s32[]{:T(128)}, f32[4,64,32]{1,0,2:T(4,128)S(1)}, f32[4,64,32]{1,0,2:T(4,128)S(1)}, f32[4,64,32,128]{3,2,1,0:T(8,128)}, f32[4,64,32]{1,0,2:T(4,128)...) while((s32[]{:T(128)}, f32[4,64,32]{1,0,2:T(4,128)S(1)}, ...), condition=%wide.region_5.6_spmd.clone, body=%wide.region_0.5_spmd.clone.sunk | while | flops 2289217536 | bytes 81249280 | solution.py:88
  10.7 7.2 %fusion.82 = (f32[4,512]{1,0:T(4,128)S(1)}, f32[4,512,2048]{2,1,0:T(8,128)}) fusion(pred[2048]{0:T(1024)(128)(4,1)S(1)} %add_compare_fusion.2, bf16[1,2048,4,128]{3,2,1,0:T(4,128)(2,1)S(1)} %constant_dynamic-slice_fusion.9, bf16[4,64,32,128]{3,2,1,0:T(8,128)(2,1)S(1)} %copy-done, s32[]{:T(128)S(6)} %copy.154), kind=kOutput, calls=%fused_computation.3.clone.1 | convolution fusion | flops 1086322688 | bytes 19408900 | tf_op jit(solution)/shard_map/while/body/eval_jaxpr/kqd,pkd->kqp/dot_general | solution.py:34
  18.2 8.1 %fusion.83 = f32[4,512]{1,0:T(4,128)S(1)} fusion(f32[4,512,2048]{2,1,0:T(8,128)} %get-tuple-element.325, f32[4,512]{1,0:T(4,128)S(1)} %get-tuple-element.324, pred[2048]{0:T(1024)(128)(4,1)S(1)} %add_compare_fusion.2), kind=kLoop, calls=%fused_computation.5.clone.1 | loop fusion | flops 20969472 | bytes 16795648 | tf_op jit(solution)/shard_map/while/body/eval_jaxpr/reduce_sum | solution.py:40
  33.0 7.7 %fusion.87 = f32[64,4,8,128]{3,2,0,1:T(8,128)S(1)} fusion(bf16[1,2048,4,128]{3,2,1,0:T(4,128)(2,1)S(1)} %constant_dynamic-slice_fusion.12, f32[4,512,2048]{2,1,0:T(8,128)} %get-tuple-element.325, f32[4,512]{1,0:T(4,128)S(1)} %get-tuple-element.324, pred[2048]{0:T(1024)(128)(4,1)S(1)} %add_compare_fusion.2), kind=kOutput, calls=%fused_computation.11.clone.1 | convolution fusion | flops 1094713344 | bytes 19933184 | tf_op jit(solution)/shard_map/while/body/eval_jaxpr/kqp,pkd->kqd/dot_general | solution.py:41
  47.2 7.2 %fusion.82 = (f32[4,512]{1,0:T(4,128)S(1)}, f32[4,512,2048]{2,1,0:T(8,128)}) fusion(pred[2048]{0:T(1024)(128)(4,1)S(1)} %add_compare_fusion.2, bf16[1,2048,4,128]{3,2,1,0:T(4,128)(2,1)S(1)} %constant_dynamic-slice_fusion.9, bf16[4,64,32,128]{3,2,1,0:T(8,128)(2,1)S(1)} %copy-done, s32[]{:T(128)S(6)} %copy.154), kind=kOutput, calls=%fused_computation.3.clone.1 | convolution fusion | flops 1086322688 | bytes 19408900 | tf_op jit(solution)/shard_map/while/body/eval_jaxpr/kqd,pkd->kqp/dot_general | solution.py:34
  54.7 8.1 %fusion.83 = f32[4,512]{1,0:T(4,128)S(1)} fusion(f32[4,512,2048]{2,1,0:T(8,128)} %get-tuple-element.325, f32[4,512]{1,0:T(4,128)S(1)} %get-tuple-element.324, pred[2048]{0:T(1024)(128)(4,1)S(1)} %add_compare_fusion.2), kind=kLoop, calls=%fused_computation.5.clone.1 | loop fusion | flops 20969472 | bytes 16795648 | tf_op jit(solution)/shard_map/while/body/eval_jaxpr/reduce_sum | solution.py:40
  69.5 7.7 %fusion.87 = f32[64,4,8,128]{3,2,0,1:T(8,128)S(1)} fusion(bf16[1,2048,4,128]{3,2,1,0:T(4,128)(2,1)S(1)} %constant_dynamic-slice_fusion.12, f32[4,512,2048]{2,1,0:T(8,128)} %get-tuple-element.325, f32[4,512]{1,0:T(4,128)S(1)} %get-tuple-element.324, pred[2048]{0:T(1024)(128)(4,1)S(1)} %add_compare_fusion.2), kind=kOutput, calls=%fused_computation.11.clone.1 | convolution fusion | flops 1094713344 | bytes 19933184 | tf_op jit(solution)/shard_map/while/body/eval_jaxpr/kqp,pkd->kqd/dot_general | solution.py:41
  83.7 7.2 %fusion.82 = (f32[4,512]{1,0:T(4,128)S(1)}, f32[4,512,2048]{2,1,0:T(8,128)}) fusion(pred[2048]{0:T(1024)(128)(4,1)S(1)} %add_compare_fusion.2, bf16[1,2048,4,128]{3,2,1,0:T(4,128)(2,1)S(1)} %constant_dynamic-slice_fusion.9, bf16[4,64,32,128]{3,2,1,0:T(8,128)(2,1)S(1)} %copy-done, s32[]{:T(128)S(6)} %copy.154), kind=kOutput, calls=%fused_computation.3.clone.1 | convolution fusion | flops 1086322688 | bytes 19408900 | tf_op jit(solution)/shard_map/while/body/eval_jaxpr/kqd,pkd->kqp/dot_general | solution.py:34
  91.2 8.1 %fusion.83 = f32[4,512]{1,0:T(4,128)S(1)} fusion(f32[4,512,2048]{2,1,0:T(8,128)} %get-tuple-element.325, f32[4,512]{1,0:T(4,128)S(1)} %get-tuple-element.324, pred[2048]{0:T(1024)(128)(4,1)S(1)} %add_compare_fusion.2), kind=kLoop, calls=%fused_computation.5.clone.1 | loop fusion | flops 20969472 | bytes 16795648 | tf_op jit(solution)/shard_map/while/body/eval_jaxpr/reduce_sum | solution.py:40
  105.9 7.7 %fusion.87 = f32[64,4,8,128]{3,2,0,1:T(8,128)S(1)} fusion(bf16[1,2048,4,128]{3,2,1,0:T(4,128)(2,1)S(1)} %constant_dynamic-slice_fusion.12, f32[4,512,2048]{2,1,0:T(8,128)} %get-tuple-element.325, f32[4,512]{1,0:T(4,128)S(1)} %get-tuple-element.324, pred[2048]{0:T(1024)(128)(4,1)S(1)} %add_compare_fusion.2), kind=kOutput, calls=%fused_computation.11.clone.1 | convolution fusion | flops 1094713344 | bytes 19933184 | tf_op jit(solution)/shard_map/while/body/eval_jaxpr/kqp,pkd->kqd/dot_general | solution.py:41
  120.1 7.2 %fusion.82 = (f32[4,512]{1,0:T(4,128)S(1)}, f32[4,512,2048]{2,1,0:T(8,128)}) fusion(pred[2048]{0:T(1024)(128)(4,1)S(1)} %add_compare_fusion.2, bf16[1,2048,4,128]{3,2,1,0:T(4,128)(2,1)S(1)} %constant_dynamic-slice_fusion.9, bf16[4,64,32,128]{3,2,1,0:T(8,128)(2,1)S(1)} %copy-done, s32[]{:T(128)S(6)} %copy.154), kind=kOutput, calls=%fused_computation.3.clone.1 | convolution fusion | flops 1086322688 | bytes 19408900 | tf_op jit(solution)/shard_map/while/body/eval_jaxpr/kqd,pkd->kqp/dot_general | solution.py:34
  127.6 8.1 %fusion.83 = f32[4,512]{1,0:T(4,128)S(1)} fusion(f32[4,512,2048]{2,1,0:T(8,128)} %get-tuple-element.325, f32[4,512]{1,0:T(4,128)S(1)} %get-tuple-element.324, pred[2048]{0:T(1024)(128)(4,1)S(1)} %add_compare_fusion.2), kind=kLoop, calls=%fused_computation.5.clone.1 | loop fusion | flops 20969472 | bytes 16795648 | tf_op jit(solution)/shard_map/while/body/eval_jaxpr/reduce_sum | solution.py:40
  142.4 7.7 %fusion.87 = f32[64,4,8,128]{3,2,0,1:T(8,128)S(1)} fusion(bf16[1,2048,4,128]{3,2,1,0:T(4,128)(2,1)S(1)} %constant_dynamic-slice_fusion.12, f32[4,512,2048]{2,1,0:T(8,128)} %get-tuple-element.325, f32[4,512]{1,0:T(4,128)S(1)} %get-tuple-element.324, pred[2048]{0:T(1024)(128)(4,1)S(1)} %add_compare_fusion.2), kind=kOutput, calls=%fused_computation.11.clone.1 | convolution fusion | flops 1094713344 | bytes 19933184 | tf_op jit(solution)/shard_map/while/body/eval_jaxpr/kqp,pkd->kqd/dot_general | solution.py:41
  152.6 63.0 %pmax.7 = f32[256,32]{0,1:T(8,128)S(1)} all-reduce(f32[256,32]{0,1:T(8,128)S(1)} %reshape.69), channel_id=1, replica_groups=mesh['seq'=16,'head'=2] {'seq'}, use_global_device_ids=true, to_apply=%region_6.7 | all-reduce | flops 8192 | bytes 65536 | tf_op jit(solution)/shard_map/pmax | solution.py:97
  221.0 48.5 %reduce-scatter.10.cloned.1.call-done = f32[16,32]{1,0:T(8,128)} async-done(((f32[256,32]{1,0:T(8,128)}), f32[16,32]{1,0:T(8,128)}) %reduce-scatter.10.cloned.1.call-update) | async-done | bytes 2064
  270.5 74.8 %reduce-scatter.6.cloned.1.call-done = f32[16,32,128]{2,1,0:T(8,128)} async-done(((f32[256,32,128]{2,1,0:T(8,128)}), f32[16,32,128]{2,1,0:T(8,128)}) %reduce-scatter.6.cloned.1.call-update) | async-done | bytes 262160 | tf_op jit(solution)/shard_map/reduce_scatter | solution.py:101
  353.7 7.1 %collective-permute-done.1 = bf16[16,4096]{1,0:T(8,128)(2,1)S(1)} collective-permute-done((bf16[16,4096]{1,0:T(8,128)(2,1)S(1)}, bf16[16,4096]{1,0:T(8,128)(2,1)S(1)}, u32[]{:S(2)}, u32[]{:S(2)}) %collective-permute-start.1) | collective-permute-done | bytes 131104 | tf_op jit(solution)/shard_map/ppermute | solution.py:15
  360.8 7.1 %collective-permute-done.2 = bf16[16,4096]{1,0:T(8,128)(2,1)S(1)} collective-permute-done((bf16[16,4096]{1,0:T(8,128)(2,1)S(1)}, bf16[16,4096]{1,0:T(8,128)(2,1)S(1)}, u32[]{:S(2)}, u32[]{:S(2)}) %collective-permute-start.2) | collective-permute-done | bytes 131104 | tf_op jit(solution)/shard_map/ppermute | solution.py:15
  367.9 7.1 %collective-permute-done.3 = bf16[16,4096]{1,0:T(8,128)(2,1)S(1)} collective-permute-done((bf16[16,4096]{1,0:T(8,128)(2,1)S(1)}, bf16[16,4096]{1,0:T(8,128)(2,1)S(1)}, u32[]{:S(2)}, u32[]{:S(2)}) %collective-permute-start.3) | collective-permute-done | bytes 131104 | tf_op jit(solution)/shard_map/ppermute | solution.py:15
  375.0 7.1 %collective-permute-done.4 = bf16[16,4096]{1,0:T(8,128)(2,1)S(1)} collective-permute-done((bf16[16,4096]{1,0:T(8,128)(2,1)S(1)}, bf16[16,4096]{1,0:T(8,128)(2,1)S(1)}, u32[]{:S(2)}, u32[]{:S(2)}) %collective-permute-start.4) | collective-permute-done | bytes 131104 | tf_op jit(solution)/shard_map/ppermute | solution.py:15
  382.1 7.1 %collective-permute-done.5 = bf16[16,4096]{1,0:T(8,128)(2,1)S(1)} collective-permute-done((bf16[16,4096]{1,0:T(8,128)(2,1)S(1)}, bf16[16,4096]{1,0:T(8,128)(2,1)S(1)}, u32[]{:S(2)}, u32[]{:S(2)}) %collective-permute-start.5) | collective-permute-done | bytes 131104 | tf_op jit(solution)/shard_map/ppermute | solution.py:15
  410.4 7.1 %collective-permute-done.9 = bf16[16,4096]{1,0:T(8,128)(2,1)S(1)} collective-permute-done((bf16[16,4096]{1,0:T(8,128)(2,1)S(1)}, bf16[16,4096]{1,0:T(8,128)(2,1)S(1)}, u32[]{:S(2)}, u32[]{:S(2)}) %collective-permute-start.9) | collective-permute-done | bytes 131104 | tf_op jit(solution)/shard_map/ppermute | solution.py:15
  431.7 7.1 %collective-permute-done.12 = bf16[16,4096]{1,0:T(8,128)(2,1)S(1)} collective-permute-done((bf16[16,4096]{1,0:T(8,128)(2,1)S(1)}, bf16[16,4096]{1,0:T(8,128)(2,1)S(1)}, u32[]{:S(2)}, u32[]{:S(2)}) %collective-permute-start.12) | collective-permute-done | bytes 131104 | tf_op jit(solution)/shard_map/ppermute | solution.py:15
  455.7 12.0 %reduce-scatter.8.cloned.1.call-done = f32[128,512]{1,0:T(8,128)} async-done(((f32[256,512]{1,0:T(8,128)}), f32[128,512]{1,0:T(8,128)}) %reduce-scatter.8.cloned.1.call-update) | async-done | bytes 262160 | tf_op jit(solution)/shard_map/reduce_scatter | solution.py:117
  (217 shorter events, 122.0 us)
Async XLA Ops:
  6.5 263.0 %reduce-scatter.10.cloned.1.call-start = ((), (), s32[]{:S(2)}) async-start(), calls=%async_computation.5 | async-start | bytes 139264
  6.6 4.2 copy-start
  43.0 4.2 copy-start
  79.5 4.2 copy-start
  115.9 4.2 copy-start
  216.5 128.8 %reduce-scatter.6.cloned.1.call-start = ((), (), s32[]{:S(2)}) async-start(), calls=%async_computation.3 | async-start | bytes 4456448 | tf_op jit(solution)/shard_map/reduce_scatter | solution.py:101
  220.8 246.9 %reduce-scatter.8.cloned.1.call-start = ((), (), s32[]{:S(2)}) async-start(), calls=%async_computation.4 | async-start | bytes 786432 | tf_op jit(solution)/shard_map/reduce_scatter | solution.py:117
  346.6 7.1 %collective-permute-start = (bf16[16,4096]{1,0:T(8,128)(2,1)S(1)}, bf16[16,4096]{1,0:T(8,128)(2,1)S(1)}, u32[]{:S(2)}, u32[]{:S(2)}) collective-permute-start(bf16[16,4096]{1,0:T(8,128)(2,1)S(1)} %bitcast.174), channel_id=1, source_target_pairs={{0,2},{2,4},{4,6},{6,8},{8,10},{10,12},{12,14},{14,16},{16,18},{18... | collective-permute-start | bytes 393224 | tf_op jit(solution)/shard_map/ppermute | solution.py:15
  353.7 7.1 %collective-permute-start.1 = (bf16[16,4096]{1,0:T(8,128)(2,1)S(1)}, bf16[16,4096]{1,0:T(8,128)(2,1)S(1)}, u32[]{:S(2)}, u32[]{:S(2)}) collective-permute-start(bf16[16,4096]{1,0:T(8,128)(2,1)S(1)} %collective-permute-done), channel_id=1, source_target_pairs={{0,2},{2,4},{4,6},{6,8},{8,10},{10,12},{12,14},{14,16},{16,18},{18... | collective-permute-start | bytes 393224 | tf_op jit(solution)/shard_map/ppermute | solution.py:15
  360.8 7.1 %collective-permute-start.2 = (bf16[16,4096]{1,0:T(8,128)(2,1)S(1)}, bf16[16,4096]{1,0:T(8,128)(2,1)S(1)}, u32[]{:S(2)}, u32[]{:S(2)}) collective-permute-start(bf16[16,4096]{1,0:T(8,128)(2,1)S(1)} %collective-permute-done.1), channel_id=1, source_target_pairs={{0,2},{2,4},{4,6},{6,8},{8,10},{10,12},{12,14},{14,16},{16,18},{18... | collective-permute-start | bytes 393224 | tf_op jit(solution)/shard_map/ppermute | solution.py:15
  367.9 7.1 %collective-permute-start.3 = (bf16[16,4096]{1,0:T(8,128)(2,1)S(1)}, bf16[16,4096]{1,0:T(8,128)(2,1)S(1)}, u32[]{:S(2)}, u32[]{:S(2)}) collective-permute-start(bf16[16,4096]{1,0:T(8,128)(2,1)S(1)} %collective-permute-done.2), channel_id=1, source_target_pairs={{0,2},{2,4},{4,6},{6,8},{8,10},{10,12},{12,14},{14,16},{16,18},{18... | collective-permute-start | bytes 393224 | tf_op jit(solution)/shard_map/ppermute | solution.py:15
  375.0 7.1 %collective-permute-start.4 = (bf16[16,4096]{1,0:T(8,128)(2,1)S(1)}, bf16[16,4096]{1,0:T(8,128)(2,1)S(1)}, u32[]{:S(2)}, u32[]{:S(2)}) collective-permute-start(bf16[16,4096]{1,0:T(8,128)(2,1)S(1)} %collective-permute-done.3), channel_id=1, source_target_pairs={{0,2},{2,4},{4,6},{6,8},{8,10},{10,12},{12,14},{14,16},{16,18},{18... | collective-permute-start | bytes 393224 | tf_op jit(solution)/shard_map/ppermute | solution.py:15
  382.1 7.1 %collective-permute-start.5 = (bf16[16,4096]{1,0:T(8,128)(2,1)S(1)}, bf16[16,4096]{1,0:T(8,128)(2,1)S(1)}, u32[]{:S(2)}, u32[]{:S(2)}) collective-permute-start(bf16[16,4096]{1,0:T(8,128)(2,1)S(1)} %collective-permute-done.4), channel_id=1, source_target_pairs={{0,2},{2,4},{4,6},{6,8},{8,10},{10,12},{12,14},{14,16},{16,18},{18... | collective-permute-start | bytes 393224 | tf_op jit(solution)/shard_map/ppermute | solution.py:15
  389.2 7.1 %collective-permute-start.6 = (bf16[16,4096]{1,0:T(8,128)(2,1)S(1)}, bf16[16,4096]{1,0:T(8,128)(2,1)S(1)}, u32[]{:S(2)}, u32[]{:S(2)}) collective-permute-start(bf16[16,4096]{1,0:T(8,128)(2,1)S(1)} %collective-permute-done.5), channel_id=1, source_target_pairs={{0,2},{2,4},{4,6},{6,8},{8,10},{10,12},{12,14},{14,16},{16,18},{18... | collective-permute-start | bytes 393224 | tf_op jit(solution)/shard_map/ppermute | solution.py:15
  396.2 7.1 %collective-permute-start.7 = (bf16[16,4096]{1,0:T(8,128)(2,1)S(1)}, bf16[16,4096]{1,0:T(8,128)(2,1)S(1)}, u32[]{:S(2)}, u32[]{:S(2)}) collective-permute-start(bf16[16,4096]{1,0:T(8,128)(2,1)S(1)} %collective-permute-done.6), channel_id=1, source_target_pairs={{0,2},{2,4},{4,6},{6,8},{8,10},{10,12},{12,14},{14,16},{16,18},{18... | collective-permute-start | bytes 393224 | tf_op jit(solution)/shard_map/ppermute | solution.py:15
  403.3 7.1 %collective-permute-start.8 = (bf16[16,4096]{1,0:T(8,128)(2,1)S(1)}, bf16[16,4096]{1,0:T(8,128)(2,1)S(1)}, u32[]{:S(2)}, u32[]{:S(2)}) collective-permute-start(bf16[16,4096]{1,0:T(8,128)(2,1)S(1)} %collective-permute-done.7), channel_id=1, source_target_pairs={{0,2},{2,4},{4,6},{6,8},{8,10},{10,12},{12,14},{14,16},{16,18},{18... | collective-permute-start | bytes 393224 | tf_op jit(solution)/shard_map/ppermute | solution.py:15
  410.4 7.1 %collective-permute-start.9 = (bf16[16,4096]{1,0:T(8,128)(2,1)S(1)}, bf16[16,4096]{1,0:T(8,128)(2,1)S(1)}, u32[]{:S(2)}, u32[]{:S(2)}) collective-permute-start(bf16[16,4096]{1,0:T(8,128)(2,1)S(1)} %collective-permute-done.8), channel_id=1, source_target_pairs={{0,2},{2,4},{4,6},{6,8},{8,10},{10,12},{12,14},{14,16},{16,18},{18... | collective-permute-start | bytes 393224 | tf_op jit(solution)/shard_map/ppermute | solution.py:15
  417.5 7.1 %collective-permute-start.10 = (bf16[16,4096]{1,0:T(8,128)(2,1)S(1)}, bf16[16,4096]{1,0:T(8,128)(2,1)S(1)}, u32[]{:S(2)}, u32[]{:S(2)}) collective-permute-start(bf16[16,4096]{1,0:T(8,128)(2,1)S(1)} %collective-permute-done.9), channel_id=1, source_target_pairs={{0,2},{2,4},{4,6},{6,8},{8,10},{10,12},{12,14},{14,16},{16,18},{18... | collective-permute-start | bytes 393224 | tf_op jit(solution)/shard_map/ppermute | solution.py:15
  424.6 7.1 %collective-permute-start.11 = (bf16[16,4096]{1,0:T(8,128)(2,1)S(1)}, bf16[16,4096]{1,0:T(8,128)(2,1)S(1)}, u32[]{:S(2)}, u32[]{:S(2)}) collective-permute-start(bf16[16,4096]{1,0:T(8,128)(2,1)S(1)} %collective-permute-done.10), channel_id=1, source_target_pairs={{0,2},{2,4},{4,6},{6,8},{8,10},{10,12},{12,14},{14,16},{16,18},{18... | collective-permute-start | bytes 393224 | tf_op jit(solution)/shard_map/ppermute | solution.py:15
  431.7 7.1 %collective-permute-start.12 = (bf16[16,4096]{1,0:T(8,128)(2,1)S(1)}, bf16[16,4096]{1,0:T(8,128)(2,1)S(1)}, u32[]{:S(2)}, u32[]{:S(2)}) collective-permute-start(bf16[16,4096]{1,0:T(8,128)(2,1)S(1)} %collective-permute-done.11), channel_id=1, source_target_pairs={{0,2},{2,4},{4,6},{6,8},{8,10},{10,12},{12,14},{14,16},{16,18},{18... | collective-permute-start | bytes 393224 | tf_op jit(solution)/shard_map/ppermute | solution.py:15
  438.8 7.1 %collective-permute-start.13 = (bf16[16,4096]{1,0:T(8,128)(2,1)S(1)}, bf16[16,4096]{1,0:T(8,128)(2,1)S(1)}, u32[]{:S(2)}, u32[]{:S(2)}) collective-permute-start(bf16[16,4096]{1,0:T(8,128)(2,1)S(1)} %collective-permute-done.12), channel_id=1, source_target_pairs={{0,2},{2,4},{4,6},{6,8},{8,10},{10,12},{12,14},{14,16},{16,18},{18... | collective-permute-start | bytes 393224 | tf_op jit(solution)/shard_map/ppermute | solution.py:15
  445.9 7.1 %collective-permute-start.14 = (bf16[16,4096]{1,0:T(8,128)(2,1)S(1)}, bf16[16,4096]{1,0:T(8,128)(2,1)S(1)}, u32[]{:S(2)}, u32[]{:S(2)}) collective-permute-start(bf16[16,4096]{1,0:T(8,128)(2,1)S(1)} %collective-permute-done.13), channel_id=1, source_target_pairs={{0,2},{2,4},{4,6},{6,8},{8,10},{10,12},{12,14},{14,16},{16,18},{18... | collective-permute-start | bytes 393224 | tf_op jit(solution)/shard_map/ppermute | solution.py:15
  445.9 7.8 %copy-start.1 = (bf16[4096,512]{1,0:T(8,128)(2,1)S(1)}, bf16[4096,512]{1,0:T(8,128)(2,1)}, u32[]{:S(2)}) copy-start(bf16[4096,512]{1,0:T(8,128)(2,1)} %param.17) | copy-start | bytes 12582916
Sparse Core Ops, SparseCore 0:
  216.6 52.8 reduce-scatter.9
  273.4 71.8 reduce-scatter.5
  455.8 11.8 reduce-scatter.7
